TPU v7x, 32 devices: a whole 2x2x4 slice. The times are simulated.
32 devices in a mesh: phase: 2 (over core), tok: 4 (over z), mp: 4 (over y, x).
Axes of the slice: x: 2, y: 2, z: 4, core: 2. Of those that a mesh axis runs over, the one named last changes fastest.
Arguments:
- hidden: bfloat16 [2, 512, 6656], P('phase', 'tok', 'mp'), may hold values from -30 to 30
- w_qkv: bfloat16 [2, 6656, 3, 4096], P('phase', 'mp', None, 'tok'), may hold values from -1 to 1
- segment_ids: int32 [2, 512], P('phase'), may hold values from 0 to 3, never falling along the last dimension, each value on 1 to 256 neighbouring positions
- exit_flags: int32 [2, 4], P('phase'), may hold values from 0 to 1, as said below
Outputs:
- attended: bfloat16 [2, 512, 4096], P('phase', 'mp', 'tok')
- handed: bfloat16 [2, 512, 4096], P('phase', 'mp', 'tok')
Inputs may be any that keep to these rules, and one draw needn't show every extreme that they name: `exit_flags`: in each micro-batch exactly 2 of the 4 blocks have flag 0.
All inputs are finite; a program needn't handle non-finite values.
Results may differ from a plain program's by a relative error of at most 0.0068.
Values may be sent and summed in bfloat16 or wider, within the bound.
A program may use at most 64 MiB of HBM per device.

v0:
```python
import math

import jax
import jax.numpy as jnp
from jax import lax
from jax.sharding import PartitionSpec as P

HEAD = 128
BLOCK = 128


def shifted(block, axis, distance):
    devices = range(lax.axis_size(axis))
    route = [((i - distance) % len(devices), i) for i in devices]
    return lax.ppermute(block, axis, route)


def attend(query, keys, values, query_pos, segment, key_pos):
    heads_here = query.shape[1] // HEAD
    total = keys.shape[0]
    key_heads = keys.reshape(total, heads_here, HEAD)
    value_heads = values.reshape(total, heads_here, HEAD)
    key_segment = jnp.take(segment, key_pos)
    scale = 1.0 / math.sqrt(HEAD)
    block_rows = query.shape[0]
    scores = (
        jnp.einsum(
            "rhd,shd->hrs",
            query.reshape(block_rows, heads_here, HEAD),
            key_heads,
            preferred_element_type=jnp.float32,
        )
        * scale
    )
    own_segment = jnp.take(segment, query_pos)
    allowed = (key_pos[None, :] <= query_pos[:, None]) & (
        key_segment[None, :] == own_segment[:, None]
    )
    scores = jnp.where(allowed[None], scores, -1e30)
    peak = jnp.max(scores, axis=-1, keepdims=True)
    expo = jnp.exp(scores - peak)
    probs = (expo / jnp.sum(expo, axis=-1, keepdims=True)).astype(jnp.bfloat16)
    mixed = jnp.einsum("hrs,shd->rhd", probs, value_heads, preferred_element_type=jnp.float32)
    return mixed.reshape(block_rows, heads_here * HEAD).astype(jnp.bfloat16)


def local(hidden, w_qkv, segment_ids, exit_flags):
    rows_here = hidden[0]
    weights = w_qkv[0]
    width_here = rows_here.shape[1]
    head_cols = weights.shape[2]
    flat_weights = weights.reshape(width_here, 3 * head_cols)
    segment = segment_ids[0]
    flags = exit_flags[0]
    groups = lax.axis_size("mp")
    member = lax.axis_index("mp")
    partial_value = jnp.dot(
        lax.all_gather(rows_here, "tok", axis=0, tiled=True),
        flat_weights,
        preferred_element_type=jnp.float32,
    )
    total = partial_value.shape[0]
    quarter = total // groups
    query_part = partial_value[:, :head_cols]
    key_value_part = partial_value[:, head_cols:]
    my_pos = member * quarter + jnp.arange(quarter, dtype=jnp.int32)
    my_blocks = my_pos // BLOCK
    alive = jnp.take(flags, my_blocks) == 0
    query = lax.psum_scatter(query_part, "mp", scatter_dimension=0, tiled=True).astype(jnp.bfloat16)
    mine = lax.psum_scatter(key_value_part, "mp", scatter_dimension=0, tiled=True).astype(
        jnp.bfloat16
    )
    key_value = lax.all_gather(mine, "mp", axis=0, tiled=True)
    all_pos = jnp.arange(total, dtype=jnp.int32)
    mixed = attend(
        query, key_value[:, :head_cols], key_value[:, head_cols:], my_pos, segment, all_pos
    )
    zeros = jnp.zeros((quarter, head_cols), jnp.bfloat16)
    result = jnp.where(alive[:, None], mixed, zeros)
    handed = shifted(result, "phase", 1)
    return (result[None], handed[None])


def solution(mesh):
    in_specs = (
        P("phase", "tok", "mp"),
        P("phase", "mp", None, "tok"),
        P("phase", None),
        P("phase", None),
    )
    out_specs = (P("phase", "mp", "tok"), P("phase", "mp", "tok"))
    return jax.shard_map(local, mesh=mesh, in_specs=in_specs, out_specs=out_specs, check_vma=False)
```

profile of v0, /device:TPU:0, one launch (start us, length us, event | category | flops | bytes accessed | tf_op | source)
XLA Modules:
  0.0 207.5 jit_solution(11496909522336261351)
XLA Ops:
  7.2 0.0 copy-start
  7.2 0.0 all-gather.6.cloned.1.call-start
  7.2 0.7 all-gather.6.cloned.1.call-update
  7.9 0.0 reduce-scatter.3.cloned.1.call-start
  8.0 13.5 %copy.11 = bf16[1,1664,3,1024]{1,3,2,0:T(8,128)(2,1)} copy(bf16[1,1664,3,1024]{3,1,2,0:T(8,128)(2,1)} %param.5) | data formatting | bytes 20447232 | tf_op args[1]
  21.5 30.0 %all-gather.6.cloned.1.call-done = bf16[1,512,1664]{2,1,0:T(8,128)(2,1)} async-done(((bf16[1,128,1664]{2,1,0:T(8,128)(2,1)}), bf16[1,512,1664]{2,1,0:T(8,128)(2,1)}) %all-gather.6.cloned.1.call-update) | async-done | bytes 1703952 | tf_op jit(solution)/shard_map/all_gather | solution.py:58
  51.5 9.1 %fusion.2 = f32[512,3072]{1,0:T(8,128)S(1)} fusion(bf16[1664,3072]{0,1:T(8,128)(2,1)} %bitcast.57, bf16[1,512,1664]{2,1,0:T(8,128)(2,1)} %all-gather.6.cloned.1.call-done), kind=kOutput, calls=%fused_computation.7 | convolution fusion | flops 5234491392 | bytes 18219008 | tf_op jit(solution)/shard_map/dot_general | solution.py:57
  60.6 0.0 copy-start.1
  60.6 2.7 %copy-done.1 = f32[512,3072]{1,0:T(8,128)} copy-done((f32[512,3072]{1,0:T(8,128)}, f32[512,3072]{1,0:T(8,128)S(1)}, u32[]{:S(2)}) %copy-start.1) | copy-done | bytes 6291480
  63.3 2.5 %slice.30 = f32[512,2048]{1,0:T(8,128)} slice(f32[512,3072]{1,0:T(8,128)S(1)} %fusion.2), slice={[0:512], [1024:3072]} | slice | bytes 8388608 | tf_op jit(solution)/shard_map/slice | solution.py:65
  65.8 0.0 reduce-scatter.3.cloned.1.call-update
  65.8 0.0 all-gather.4.cloned.1.call-start
  65.9 51.5 %reduce-scatter.3.cloned.1.call-done = f32[128,2048]{1,0:T(8,128)} async-done(((f32[512,2048]{1,0:T(8,128)}), f32[128,2048]{1,0:T(8,128)}) %reduce-scatter.3.cloned.1.call-update) | async-done | bytes 1048592 | tf_op jit(solution)/shard_map/reduce_scatter | solution.py:70
  117.4 2.1 %convert_element_type.29 = bf16[128,2048]{1,0:T(8,128)(2,1)} convert(f32[128,2048]{1,0:T(8,128)} %reduce-scatter.3.cloned.1.call-done) | non-fusion elementwise | flops 262144 | bytes 1572864 | tf_op jit(solution)/shard_map/convert_element_type | solution.py:70
  119.5 0.0 all-gather.4.cloned.1.call-update
  119.5 0.0 reduce-scatter.5.cloned.1.call-start
  119.6 3.2 %slice.32 = f32[512,1024]{1,0:T(8,128)} slice(f32[512,3072]{1,0:T(8,128)} %copy-done.1), slice={[0:512], [0:1024]} | slice | bytes 4194304 | tf_op jit(solution)/shard_map/slice | solution.py:64
  122.8 0.0 copy-start.2
  122.8 0.0 reduce-scatter.5.cloned.1.call-update
  122.8 0.0 copy-done
  122.8 3.5 %gather_fusion = s32[512]{0:T(512)S(1)} fusion(s32[512]{0:T(512)S(1)} %bitcast.55, s32[1024]{0:T(1024)S(1)} %pad_clamp_fusion.1), kind=kCustom, calls=%fused_computation | custom fusion | bytes 6144 | tf_op jit(solution)/shard_map/jit(_take)/gather | solution.py:23
  126.4 1.3 gather_fusion.1
  127.7 0.0 copy-done.2
  127.7 0.7 fusion.31
  128.3 2.6 %fusion.28 = pred[128]{0:T(512)(128)(4,1)S(1)} fusion(s32[]{:T(128)} %bitcast, s32[]{:T(128)} %bitcast.1, s32[]{:T(128)} %bitcast.3, s32[]{:T(128)} %bitcast.2, s32[]{:T(128)S(6)} %mul.9), kind=kLoop, calls=%fused_computation.48 | loop fusion | flops 6272 | bytes 148 | tf_op jit(solution)/shard_map/eq | solution.py:68
  130.9 0.1 fusion.12
  131.0 23.8 %all-gather.4.cloned.1.call-done = bf16[512,2048]{1,0:T(8,128)(2,1)} async-done(((bf16[128,2048]{1,0:T(8,128)(2,1)}), bf16[512,2048]{1,0:T(8,128)(2,1)}) %all-gather.4.cloned.1.call-update) | async-done | bytes 2097168 | tf_op jit(solution)/shard_map/all_gather | solution.py:73
  154.9 1.7 slice_bitcast_fusion
  156.6 0.5 copy.17
  157.2 35.7 %reduce-scatter.5.cloned.1.call-done = f32[128,1024]{1,0:T(8,128)} async-done(((f32[512,1024]{1,0:T(8,128)}), f32[128,1024]{1,0:T(8,128)}) %reduce-scatter.5.cloned.1.call-update) | async-done | bytes 524304 | tf_op jit(solution)/shard_map/reduce_scatter | solution.py:69
  192.9 3.3 %fusion.32 = (f32[8,128]{1,0:T(8,128)S(1)}, f32[8,128,512]{2,1,0:T(8,128)}) fusion(pred[128,512]{1,0:T(8,128)(4,1)S(1)} %fusion.12, bf16[64,8,8,128]{3,2,1,0:T(8,128)(2,1)S(1)} %get-tuple-element.2, f32[128,1024]{1,0:T(8,128)} %reduce-scatter.5.cloned.1.call-done), kind=kOutput, calls=%fused_computation.53 | convolution fusion | flops 136446464 | bytes 3739648 | tf_op jit(solution)/shard_map/sub | solution.py:41
  196.2 2.2 %convolution_convert_fusion = bf16[8,128,128]{2,1,0:T(8,128)(2,1)S(1)} fusion(bf16[512,8,128]{0,2,1:T(8,128)(2,1)S(1)} %bitcast.58, f32[8,128,512]{2,1,0:T(8,128)} %get-tuple-element.9, f32[8,128]{1,0:T(8,128)S(1)} %get-tuple-element.8), kind=kOutput, calls=%fused_computation.9 | convolution fusion | flops 135397376 | bytes 3411968 | tf_op jit(solution)/shard_map/hrs,shd->rhd/dot_general | solution.py:43
  198.4 0.1 copy.16
  198.6 0.1 broadcast_select_fusion
  198.6 0.1 collective-permute-start
  198.7 0.1 copy.15
  198.9 0.8 broadcast_select_fusion.1
  199.7 0.6 collective-permute-done
  200.2 0.7 copy.45
  (6 shorter events, 0.0 us)
Async XLA Ops:
  7.2 115.7 %copy-start = (s32[1,512]{1,0:T(1,128)S(1)}, s32[1,512]{1,0:T(1,128)}, u32[]{:S(2)}) copy-start(s32[1,512]{1,0:T(1,128)} %param.6) | copy-start | bytes 6148
  7.2 44.3 %all-gather.6.cloned.1.call-start = ((), (), s32[]{:S(2)}) async-start(), calls=%async_computation.5 | async-start | bytes 2129920 | tf_op jit(solution)/shard_map/all_gather | solution.py:58
  7.9 109.5 %reduce-scatter.3.cloned.1.call-start = ((), (), s32[]{:S(2)}) async-start(), calls=%async_computation.2 | async-start | bytes 5242880 | tf_op jit(solution)/shard_map/reduce_scatter | solution.py:70
  60.6 2.7 %copy-start.1 = (f32[512,3072]{1,0:T(8,128)}, f32[512,3072]{1,0:T(8,128)S(1)}, u32[]{:S(2)}) copy-start(f32[512,3072]{1,0:T(8,128)S(1)} %fusion.2) | copy-start | bytes 18874372
  65.8 89.1 %all-gather.4.cloned.1.call-start = ((), (), s32[]{:S(2)}) async-start(), calls=%async_computation.3 | async-start | bytes 2621440 | tf_op jit(solution)/shard_map/all_gather | solution.py:73
  119.5 73.4 %reduce-scatter.5.cloned.1.call-start = ((), (), s32[]{:S(2)}) async-start(), calls=%async_computation.4 | async-start | bytes 2621440 | tf_op jit(solution)/shard_map/reduce_scatter | solution.py:69
  122.8 4.9 %copy-start.2 = (s32[1,4]{1,0:T(1,128)S(1)}, s32[1,4]{1,0:T(1,128)}, u32[]{:S(2)}) copy-start(s32[1,4]{1,0:T(1,128)} %param.7) | copy-start | bytes 52
  198.6 1.6 collective-permute-start
Sparse Core Ops, SparseCore 0:
  9.6 41.8 all-gather.5
  65.9 51.4 reduce-scatter.2
  119.6 35.1 all-gather.3
  157.7 35.1 reduce-scatter.4
where the time goes:
time: 208 us; the launch traced here: 207 us
  waiting for transfers between devices  142 us (68%)
  local copies, waits for them, and re-layouts  30.7 us (15%)
  matrix products  14.6 us (7%)
  between operations  13.9 us (7%)
  other arithmetic  5.68 us (3%)
    reduce_scatter x1, waiting for transfers between devices, local(): lax.psum_scatter(key_value_part, 'mp', scatter_dimension=0, tiled=True)  51.5 us
    reduce_scatter x1, waiting for transfers between devices, local(): lax.psum_scatter(query_part, 'mp', scatter_dimension=0, tiled=True)  35.7 us
    all_gather x1, waiting for transfers between devices, local(): lax.all_gather(rows_here, 'tok', axis=0, tiled=True)  30 us
    all_gather x1, waiting for transfers between devices, local(): key_value = lax.all_gather(mine, 'mp', axis=0, tiled=True)  23.8 us
    unnamed x9, local copies, waits for them, and re-layouts  18.7 us
    dot_general x1, matrix products, local(): jnp.dot(lax.all_gather(rows_here, 'tok', axis=0, tiled=True), flat_weight...  9.08 us
  transfers between devices with their start and end apart: 5, of which 5 were waited for; matrix products, arithmetic and copies ran while one was open for 14% of the time, Pallas kernels for 0%

commit v1 on v0

--- a/solution.py
+++ b/solution.py
@@ -1,12 +1,300 @@
+import functools
 import math
 
 import jax
 import jax.numpy as jnp
 from jax import lax
+from jax.experimental import pallas as pl
+from jax.experimental.pallas import tpu as pltpu
 from jax.sharding import PartitionSpec as P
 
 HEAD = 128
 BLOCK = 128
+CHUNKS = 2
+MESH = pl.DeviceIdType.MESH
+
+
+def remote(src, dst, send, recv, where):
+    return pltpu.make_async_remote_copy(
+        src_ref=src, dst_ref=dst, send_sem=send, recv_sem=recv, device_id=where, device_id_type=MESH
+    )
+
+
+def fused_kernel(
+    tiers, groups, x_ref, w_ref, seg_ref, flag_ref, att_ref, hand_ref,
+    hid, wbuf, sendb, recvb, acc, qkv, outb,
+    own_sem, w_sem, up_sem, down_sem, gather_sem, rs_send, rs_recv, a_send, a_recv, h_send, h_recv,
+):
+    p = lax.axis_index("phase")
+    z = lax.axis_index("tok")
+    m = lax.axis_index("mp")
+    rows = x_ref.shape[0]
+    piece = rows // CHUNKS
+    cols = w_ref.shape[2] // groups
+    total = rows * tiers
+    quarter = total // groups
+    scale = 1.0 / math.sqrt(HEAD)
+
+    def columns(member):
+        return pl.ds(pl.multiple_of(member * cols, HEAD), cols)
+
+    own = pltpu.make_async_copy(x_ref, hid.at[z], own_sem)
+    own.start()
+
+    def weights(j):
+        dest = (m + j) % groups
+        return pltpu.make_async_copy(w_ref.at[:, :, columns(dest)], wbuf.at[j], w_sem.at[j])
+
+    for j in [*range(1, groups), 0]:
+        weights(j).start()
+
+    barrier = pltpu.get_barrier_semaphore()
+
+    @pl.when(z > 0)
+    def _():
+        pl.semaphore_signal(barrier, inc=1, device_id={"tok": z - 1}, device_id_type=MESH)
+
+    @pl.when(z < tiers - 1)
+    def _():
+        pl.semaphore_signal(barrier, inc=1, device_id={"tok": z + 1}, device_id_type=MESH)
+
+    for j in range(1, groups):
+        pl.semaphore_signal(
+            barrier, inc=1, device_id={"mp": (m + j) % groups}, device_id_type=MESH
+        )
+    pl.semaphore_signal(barrier, inc=1, device_id={"phase": 1 - p}, device_id_type=MESH)
+    pl.semaphore_wait(barrier, groups + jnp.minimum(z, 1) + jnp.minimum(tiers - 1 - z, 1))
+
+    def part(c):
+        return pl.ds(c * piece, piece)
+
+    def upward(src, t, c):
+        return remote(
+            src, hid.at[t, part(c)], up_sem.at[t, c], gather_sem.at[t, c], {"tok": z + 1}
+        )
+
+    def downward(src, t, c):
+        return remote(
+            src, hid.at[t, part(c)], down_sem.at[t, c], gather_sem.at[t, c], {"tok": z - 1}
+        )
+
+    for c in range(CHUNKS):
+
+        @pl.when(z < tiers - 1)
+        def _():
+            upward(x_ref.at[part(c)], z, c).start()
+
+        @pl.when(z > 0)
+        def _():
+            downward(x_ref.at[part(c)], z, c).start()
+
+    def relay(d):
+        for c in range(CHUNKS):
+
+            @pl.when(z - d >= 0)
+            def _():
+                t = z - d
+                src = hid.at[t, part(c)]
+                upward(src, t, c).wait_recv()
+
+                @pl.when(z < tiers - 1)
+                def _():
+                    upward(src, t, c).start()
+
+            @pl.when(z + d < tiers)
+            def _():
+                t = z + d
+                src = hid.at[t, part(c)]
+                downward(src, t, c).wait_recv()
+
+                @pl.when(z > 0)
+                def _():
+                    downward(src, t, c).start()
+
+    near = jnp.minimum(z, tiers - 1 - z)
+
+    def shard_at(s):
+        d = (s + 1) // 2
+        paired = jnp.where(s % 2 == 1, z - d, z + d)
+        far = s - near
+        single = jnp.where(z <= tiers - 1 - z, z + far, z - far)
+        return jnp.where(s <= 2 * near, paired, single)
+
+    def scatter(j, t):
+        return remote(
+            sendb.at[j - 1, t], recvb.at[j - 1, t], rs_send.at[j - 1, t], rs_recv.at[j - 1, t],
+            {"mp": (m + j) % groups},
+        )
+
+    def multiply(s, t):
+        @pl.loop(1, groups)
+        def _(j):
+            @pl.when(s == 0)
+            def _():
+                weights(j).wait()
+
+            for c in range(3):
+                got = jnp.dot(hid[t], wbuf[j, c], preferred_element_type=jnp.float32)
+                sendb[j - 1, t, :, c * cols : (c + 1) * cols] = got.astype(jnp.bfloat16)
+            scatter(j, t).start()
+
+        @pl.when(s == 0)
+        def _():
+            weights(0).wait()
+
+        for c in range(3):
+            acc[t, :, c * cols : (c + 1) * cols] = jnp.dot(
+                hid[t], wbuf[0, c], preferred_element_type=jnp.float32
+            )
+
+    def finish(t):
+        for j in range(1, groups):
+            scatter(j, t).wait_recv()
+        for c in range(3):
+            span = slice(c * cols, (c + 1) * cols)
+            value = acc[t, :, span]
+            for j in range(1, groups):
+                value = value + recvb[j - 1, t, :, span].astype(jnp.float32)
+            qkv[c, pl.ds(pl.multiple_of(t * rows, rows), rows), :] = value.astype(jnp.bfloat16)
+
+    own.wait()
+
+    @pl.loop(0, tiers)
+    def _(s):
+        @pl.when(s > 0)
+        def _():
+            relay(s)
+
+        multiply(s, shard_at(s))
+
+        @pl.when(s > 0)
+        def _():
+            finish(shard_at(s - 1))
+
+    finish(shard_at(tiers - 1))
+
+    def exchange(j):
+        return remote(
+            outb.at[j - 1], att_ref.at[:, columns(m)], a_send.at[j - 1], a_recv.at[j - 1],
+            {"mp": (m + j) % groups},
+        )
+
+    def hand(j, member, src):
+        return remote(
+            src, hand_ref.at[:, columns(member)], h_send.at[j - 1], h_recv.at[j - 1],
+            {"phase": 1 - p},
+        )
+
+    seg_keys = seg_ref[...]
+    key_pos = lax.broadcasted_iota(jnp.int32, (BLOCK, total), 1)
+    row_pos = lax.broadcasted_iota(jnp.int32, (BLOCK, total), 0)
+
+    @pl.loop(1, groups + 1)
+    def _(j):
+        r = (m + j) % groups
+        for b in range(quarter // BLOCK):
+            first = pl.multiple_of(r * quarter + b * BLOCK, BLOCK)
+            here = pl.ds(first, BLOCK)
+            seg_rows = jnp.broadcast_to(seg_ref[:, here], (BLOCK, BLOCK)).T
+            seg_rows = jnp.concatenate([seg_rows] * (total // BLOCK), axis=1)
+            allowed = (key_pos <= row_pos + first) & (seg_rows == seg_keys)
+            flag = flag_ref[0, r * (quarter // BLOCK) + b]
+            kept = jnp.full((BLOCK, HEAD), flag, jnp.int32) == 0
+            for h in range(cols // HEAD):
+                head = slice(h * HEAD, (h + 1) * HEAD)
+                scores = (
+                    lax.dot_general(
+                        qkv[0, here, head], qkv[1, :, head], (((1,), (1,)), ((), ())),
+                        preferred_element_type=jnp.float32,
+                    )
+                    * scale
+                )
+                scores = jnp.where(allowed, scores, -1e30)
+                peak = jnp.max(scores, axis=-1, keepdims=True)
+                expo = jnp.exp(scores - peak)
+                probs = (expo / jnp.sum(expo, axis=-1, keepdims=True)).astype(jnp.bfloat16)
+                mixed = jnp.dot(probs, qkv[2, :, head], preferred_element_type=jnp.float32)
+                outb[j - 1, b * BLOCK : (b + 1) * BLOCK, head] = jnp.where(
+                    kept, mixed, 0.0
+                ).astype(jnp.bfloat16)
+
+        @pl.when(j < groups)
+        def _():
+            exchange(j).start()
+
+    hand(groups, m, outb.at[groups - 1]).start()
+    att_ref[:, columns(m)] = outb[groups - 1]
+    for j in range(1, groups):
+        member = (m + groups - j) % groups
+        exchange(j).wait_recv()
+        hand(j, member, att_ref.at[:, columns(member)]).start()
+
+    for c in range(CHUNKS):
+        for t in range(tiers):
+
+            @pl.when((z >= t) & (z < tiers - 1))
+            def _():
+                upward(hid.at[t, part(c)], t, c).wait_send()
+
+            @pl.when((z <= t) & (z > 0))
+            def _():
+                downward(hid.at[t, part(c)], t, c).wait_send()
+
+    for j in range(1, groups):
+        for t in range(tiers):
+            scatter(j, t).wait_send()
+        exchange(j).wait_send()
+    for j in range(1, groups + 1):
+        hand(j, m, outb.at[groups - 1]).wait()
+
+
+def local_fused(hidden, w_qkv, segment_ids, exit_flags):
+    rows = hidden[0]
+    weights = jnp.transpose(w_qkv[0], (1, 0, 2))
+    tiers = lax.axis_size("tok")
+    groups = lax.axis_size("mp")
+    count, width = rows.shape
+    head_cols = weights.shape[2]
+    cols = head_cols // groups
+    total = count * tiers
+    quarter = total // groups
+    out = jax.ShapeDtypeStruct((quarter, head_cols), jnp.bfloat16)
+    dma = pltpu.SemaphoreType.DMA
+    attended, handed = pl.pallas_call(
+        functools.partial(fused_kernel, tiers, groups),
+        out_shape=(out, out),
+        in_specs=[
+            pl.BlockSpec(memory_space=pl.ANY),
+            pl.BlockSpec(memory_space=pl.ANY),
+            pl.BlockSpec(memory_space=pltpu.VMEM),
+            pl.BlockSpec(memory_space=pltpu.SMEM),
+        ],
+        out_specs=(pl.BlockSpec(memory_space=pltpu.VMEM),) * 2,
+        scratch_shapes=[
+            pltpu.VMEM((tiers, count, width), jnp.bfloat16),
+            pltpu.VMEM((groups, 3, width, cols), jnp.bfloat16),
+            pltpu.VMEM((groups - 1, tiers, count, 3 * cols), jnp.bfloat16),
+            pltpu.VMEM((groups - 1, tiers, count, 3 * cols), jnp.bfloat16),
+            pltpu.VMEM((tiers, count, 3 * cols), jnp.float32),
+            pltpu.VMEM((3, total, cols), jnp.bfloat16),
+            pltpu.VMEM((groups, quarter, cols), jnp.bfloat16),
+            dma(()),
+            dma((groups,)),
+            dma((tiers, CHUNKS)),
+            dma((tiers, CHUNKS)),
+            dma((tiers, CHUNKS)),
+            dma((groups - 1, tiers)),
+            dma((groups - 1, tiers)),
+            dma((groups - 1,)),
+            dma((groups - 1,)),
+            dma((groups,)),
+            dma((groups,)),
+        ],
+        compiler_params=pltpu.CompilerParams(
+            collective_id=0, has_side_effects=True, vmem_limit_bytes=60 * 1024 * 1024
+        ),
+    )(rows, weights, segment_ids, exit_flags)
+    return (attended[None], handed[None])
 
 
 def shifted(block, axis, distance):
@@ -89,4 +377,15 @@
         P("phase", None),
     )
     out_specs = (P("phase", "mp", "tok"), P("phase", "mp", "tok"))
-    return jax.shard_map(local, mesh=mesh, in_specs=in_specs, out_specs=out_specs, check_vma=False)
+    sizes = dict(mesh.shape)
+
+    def step(hidden, w_qkv, segment_ids, exit_flags):
+        heads_here = w_qkv.shape[3] // sizes["tok"] // HEAD
+        quarter = hidden.shape[1] // sizes["mp"]
+        by_head = heads_here % sizes["mp"] == 0 and quarter % BLOCK == 0 and sizes["phase"] == 2
+        body = local_fused if by_head else local
+        return jax.shard_map(
+            body, mesh=mesh, in_specs=in_specs, out_specs=out_specs, check_vma=False
+        )(hidden, w_qkv, segment_ids, exit_flags)
+
+    return step

time: 208 us -> 57.2 us (0.28)
  waiting for transfers between devices: 142 us -> 0 us
  Pallas kernels: 0 us -> 53.1 us
  local copies, waits for them, and re-layouts: 30.7 us -> 3.34 us
  matrix products: 14.6 us -> 0 us
  between operations: 13.9 us -> 0.64 us
  other arithmetic: 5.68 us -> 0 us
    reduce_scatter x2 -> x0, waiting for transfers between devices: 87.3 us -> none  [the longest x1 51.5 us: local(): lax.psum_scatter(key_value_part, 'mp', scatter_dimension=0, tiled=True)]
    all_gather x2 -> x0, waiting for transfers between devices: 53.8 us -> none  [the longest x1 30 us: local(): lax.all_gather(rows_here, 'tok', axis=0, tiled=True)]
    pallas_call x0 -> x1, Pallas kernels: none -> 53.1 us  [local_fused(): pl.pallas_call(functools.partial(fused_kernel, tiers, groups), out_shape=...]
    unnamed x9 -> x2, local copies, waits for them, and re-layouts: 18.7 us -> 3.34 us
    dot_general x2 -> x0, matrix products: 11.2 us -> none  [the longest x1 9.08 us: local(): jnp.dot(lax.all_gather(rows_here, 'tok', axis=0, tiled=True), flat_weight...]
    slice x2 -> x0, local copies, waits for them, and re-layouts: 5.73 us -> none  [the longest x1 3.21 us: local(): query_part = partial_value[:, :head_cols]]
    gather x3 -> x0, local copies, waits for them, and re-layouts: 5.43 us -> none  [the longest x1 3.51 us: attend(): key_segment = jnp.take(segment, key_pos)]
    sub x1 -> x0, matrix products: 3.33 us -> none  [attend(): expo = jnp.exp(scores - peak)]
  transfers between devices with their start and end apart: 5 -> 0, of which waited for: 5 -> 0; matrix products, arithmetic and copies ran while one was open for 14% -> 0% of each run, Pallas kernels for 0% -> 0%
where the time goes in v1:
time: 57.2 us; the launch traced here: 57 us
  Pallas kernels  53.1 us (93%)
  local copies, waits for them, and re-layouts  3.34 us (6%)
  between operations  0.64 us (1%)
    pallas_call x1, Pallas kernels, local_fused(): pl.pallas_call(functools.partial(fused_kernel, tiers, groups), out_shape=...  53.1 us
    unnamed x2, local copies, waits for them, and re-layouts  3.34 us

profile of v1, /device:TPU:0, one launch (start us, length us, event | category | flops | bytes accessed | tf_op | source)
XLA Modules:
  0.0 57.0 jit_solution(4503795660583086049)
XLA Ops:
  0.6 53.1 %shard_map.59 = (bf16[128,1024]{1,0:T(8,128)(2,1)}, bf16[128,1024]{1,0:T(8,128)(2,1)}) custom-call(bf16[128,1664]{1,0:T(8,128)(2,1)} %bitcast.7, bf16[3,1664,1024]{2,1,0:T(8,128)(2,1)} %bitcast.6, s32[1,512]{1,0:T(1,128)} %seg_ref.1, s32[1,4]{1,0:T(1,128)} %flag_ref.1), custom_call_target="tpu_custom_call" | custom-call | tf_op jit(solution)/shard_map/pallas_call | solution.py:263
  53.7 1.7 %copy.8 = bf16[1,128,1024]{2,1,0:T(8,128)(2,1)} copy(bf16[1,128,1024]{2,1,0:T(8,128)(2,1)} %bitcast.9) | data formatting | bytes 524288
  55.4 1.7 %copy.9 = bf16[1,128,1024]{2,1,0:T(8,128)(2,1)} copy(bf16[1,128,1024]{2,1,0:T(8,128)(2,1)} %bitcast.8) | data formatting | bytes 524288

commit v2 on v1

--- a/solution.py
+++ b/solution.py
@@ -22,7 +22,7 @@
 
 def fused_kernel(
     tiers, groups, x_ref, w_ref, seg_ref, flag_ref, att_ref, hand_ref,
-    hid, wbuf, sendb, recvb, acc, qkv, outb,
+    hid, wbuf, sendb, recvb, acc, qkv, outb, pend,
     own_sem, w_sem, up_sem, down_sem, gather_sem, rs_send, rs_recv, a_send, a_recv, h_send, h_recv,
 ):
     p = lax.axis_index("phase")
@@ -35,6 +35,12 @@
     quarter = total // groups
     scale = 1.0 / math.sqrt(HEAD)
 
+    half = 3 * cols // 2
+    halves = (slice(0, half), slice(half, 3 * cols))
+
+    def peer(j):
+        return (m // 2 + j // 2) % 2 * 2 + (m % 2 + j % 2) % 2
+
     def columns(member):
         return pl.ds(pl.multiple_of(member * cols, HEAD), cols)
 
@@ -42,10 +48,10 @@
     own.start()
 
     def weights(j):
-        dest = (m + j) % groups
+        dest = peer(j)
         return pltpu.make_async_copy(w_ref.at[:, :, columns(dest)], wbuf.at[j], w_sem.at[j])
 
-    for j in [*range(1, groups), 0]:
+    for j in (3, 1, 2, 0):
         weights(j).start()
 
     barrier = pltpu.get_barrier_semaphore()
@@ -60,13 +66,13 @@
 
     for j in range(1, groups):
         pl.semaphore_signal(
-            barrier, inc=1, device_id={"mp": (m + j) % groups}, device_id_type=MESH
+            barrier, inc=1, device_id={"mp": peer(j)}, device_id_type=MESH
         )
     pl.semaphore_signal(barrier, inc=1, device_id={"phase": 1 - p}, device_id_type=MESH)
     pl.semaphore_wait(barrier, groups + jnp.minimum(z, 1) + jnp.minimum(tiers - 1 - z, 1))
 
     def part(c):
-        return pl.ds(c * piece, piece)
+        return pl.ds(pl.multiple_of(c * piece, piece), piece)
 
     def upward(src, t, c):
         return remote(
@@ -88,28 +94,26 @@
         def _():
             downward(x_ref.at[part(c)], z, c).start()
 
-    def relay(d):
-        for c in range(CHUNKS):
-
-            @pl.when(z - d >= 0)
+    def relay(d, c):
+        @pl.when(z - d >= 0)
+        def _():
+            t = z - d
+            src = hid.at[t, part(c)]
+            upward(src, t, c).wait_recv()
+
+            @pl.when(z < tiers - 1)
             def _():
-                t = z - d
-                src = hid.at[t, part(c)]
-                upward(src, t, c).wait_recv()
-
-                @pl.when(z < tiers - 1)
-                def _():
-                    upward(src, t, c).start()
-
-            @pl.when(z + d < tiers)
+                upward(src, t, c).start()
+
+        @pl.when(z + d < tiers)
+        def _():
+            t = z + d
+            src = hid.at[t, part(c)]
+            downward(src, t, c).wait_recv()
+
+            @pl.when(z > 0)
             def _():
-                t = z + d
-                src = hid.at[t, part(c)]
-                downward(src, t, c).wait_recv()
-
-                @pl.when(z > 0)
-                def _():
-                    downward(src, t, c).start()
+                downward(src, t, c).start()
 
     near = jnp.minimum(z, tiers - 1 - z)
 
@@ -120,63 +124,87 @@
         single = jnp.where(z <= tiers - 1 - z, z + far, z - far)
         return jnp.where(s <= 2 * near, paired, single)
 
-    def scatter(j, t):
+    def scatter(j, t, c, h):
+        where = peer(j) if j < 3 else peer(2 - h)
         return remote(
-            sendb.at[j - 1, t], recvb.at[j - 1, t], rs_send.at[j - 1, t], rs_recv.at[j - 1, t],
-            {"mp": (m + j) % groups},
-        )
-
-    def multiply(s, t):
-        @pl.loop(1, groups)
-        def _(j):
-            @pl.when(s == 0)
-            def _():
-                weights(j).wait()
-
-            for c in range(3):
-                got = jnp.dot(hid[t], wbuf[j, c], preferred_element_type=jnp.float32)
-                sendb[j - 1, t, :, c * cols : (c + 1) * cols] = got.astype(jnp.bfloat16)
-            scatter(j, t).start()
-
-        @pl.when(s == 0)
-        def _():
-            weights(0).wait()
-
-        for c in range(3):
-            acc[t, :, c * cols : (c + 1) * cols] = jnp.dot(
-                hid[t], wbuf[0, c], preferred_element_type=jnp.float32
-            )
-
-    def finish(t):
-        for j in range(1, groups):
-            scatter(j, t).wait_recv()
-        for c in range(3):
-            span = slice(c * cols, (c + 1) * cols)
-            value = acc[t, :, span]
-            for j in range(1, groups):
-                value = value + recvb[j - 1, t, :, span].astype(jnp.float32)
-            qkv[c, pl.ds(pl.multiple_of(t * rows, rows), rows), :] = value.astype(jnp.bfloat16)
+            sendb.at[j - 1, t, part(c), halves[h]], recvb.at[j - 1, t, part(c), halves[h]],
+            rs_send.at[j - 1, t, c, h], rs_recv.at[j - 1, t, c, h], {"mp": where},
+        )
+
+    def product(n, t, c, j):
+        @pl.when(n == 0)
+        def _():
+            weights(j).wait()
+
+        return [
+            jnp.dot(hid[t, part(c), :], wbuf[j, k], preferred_element_type=jnp.float32)
+            for k in range(3)
+        ]
+
+    def multiply(n, t, c):
+        got = jnp.concatenate(product(n, t, c, 3), axis=1)
+        sendb[2, t, part(c), :] = got.astype(jnp.bfloat16)
+        scatter(3, t, c, 0).start()
+        scatter(3, t, c, 1).start()
+        for j in (1, 2):
+            held, direct = halves[j - 1], halves[2 - j]
+            got = jnp.concatenate(product(n, t, c, j), axis=1)
+            sendb[j - 1, t, part(c), direct] = got[:, direct].astype(jnp.bfloat16)
+            scatter(j, t, c, 2 - j).start()
+            pend[t, part(c), held] = got[:, held]
+        acc[t, part(c), :] = jnp.concatenate(product(n, t, c, 0), axis=1)
+
+    def combine(t, c):
+        for j in (1, 2):
+            held = halves[j - 1]
+            scatter(3, t, c, j - 1).wait_recv()
+            total_here = pend[t, part(c), held] + recvb[2, t, part(c), held].astype(jnp.float32)
+            sendb[j - 1, t, part(c), held] = total_here.astype(jnp.bfloat16)
+            scatter(j, t, c, j - 1).start()
+
+    def finish(t, c):
+        for j in (1, 2):
+            for h in range(2):
+                scatter(j, t, c, h).wait_recv()
+        first = pl.multiple_of(t * rows + c * piece, piece)
+        for k in range(3):
+            span = slice(k * cols, (k + 1) * cols)
+            value = acc[t, part(c), span]
+            for j in (1, 2):
+                value = value + recvb[j - 1, t, part(c), span].astype(jnp.float32)
+            qkv[k, pl.ds(first, piece), :] = value.astype(jnp.bfloat16)
+
+    steps = tiers * CHUNKS
+
+    def at(n):
+        return shard_at(n // CHUNKS), n % CHUNKS
 
     own.wait()
 
-    @pl.loop(0, tiers)
-    def _(s):
-        @pl.when(s > 0)
-        def _():
-            relay(s)
-
-        multiply(s, shard_at(s))
-
-        @pl.when(s > 0)
-        def _():
-            finish(shard_at(s - 1))
-
-    finish(shard_at(tiers - 1))
+    @pl.loop(0, steps)
+    def _(n):
+        @pl.when(n >= CHUNKS)
+        def _():
+            relay(n // CHUNKS, n % CHUNKS)
+
+        multiply(n, *at(n))
+
+        @pl.when(n > 0)
+        def _():
+            combine(*at(n - 1))
+
+        @pl.when(n > 1)
+        def _():
+            finish(*at(n - 2))
+
+    combine(*at(steps - 1))
+    finish(*at(steps - 2))
+    finish(*at(steps - 1))
 
     def exchange(j):
         return remote(
             outb.at[j - 1], att_ref.at[:, columns(m)], a_send.at[j - 1], a_recv.at[j - 1],
-            {"mp": (m + j) % groups},
+            {"mp": peer(j)},
         )
 
     def hand(j, member, src):
@@ -191,7 +219,7 @@
 
     @pl.loop(1, groups + 1)
     def _(j):
-        r = (m + j) % groups
+        r = peer(j)
         for b in range(quarter // BLOCK):
             first = pl.multiple_of(r * quarter + b * BLOCK, BLOCK)
             here = pl.ds(first, BLOCK)
@@ -225,7 +253,7 @@
     hand(groups, m, outb.at[groups - 1]).start()
     att_ref[:, columns(m)] = outb[groups - 1]
     for j in range(1, groups):
-        member = (m + groups - j) % groups
+        member = peer(j)
         exchange(j).wait_recv()
         hand(j, member, att_ref.at[:, columns(member)]).start()
 
@@ -242,7 +270,9 @@
 
     for j in range(1, groups):
         for t in range(tiers):
-            scatter(j, t).wait_send()
+            for c in range(CHUNKS):
+                for h in range(2):
+                    scatter(j, t, c, h).wait_send()
         exchange(j).wait_send()
     for j in range(1, groups + 1):
         hand(j, m, outb.at[groups - 1]).wait()
@@ -278,13 +308,14 @@
             pltpu.VMEM((tiers, count, 3 * cols), jnp.float32),
             pltpu.VMEM((3, total, cols), jnp.bfloat16),
             pltpu.VMEM((groups, quarter, cols), jnp.bfloat16),
+            pltpu.VMEM((tiers, count, 3 * cols), jnp.float32),
             dma(()),
             dma((groups,)),
             dma((tiers, CHUNKS)),
             dma((tiers, CHUNKS)),
             dma((tiers, CHUNKS)),
-            dma((groups - 1, tiers)),
-            dma((groups - 1, tiers)),
+            dma((groups - 1, tiers, CHUNKS, 2)),
+            dma((groups - 1, tiers, CHUNKS, 2)),
             dma((groups - 1,)),
             dma((groups - 1,)),
             dma((groups,)),
@@ -383,6 +414,7 @@
         heads_here = w_qkv.shape[3] // sizes["tok"] // HEAD
         quarter = hidden.shape[1] // sizes["mp"]
         by_head = heads_here % sizes["mp"] == 0 and quarter % BLOCK == 0 and sizes["phase"] == 2
+        by_head = by_head and sizes["mp"] == 4
         body = local_fused if by_head else local
         return jax.shard_map(
             body, mesh=mesh, in_specs=in_specs, out_specs=out_specs, check_vma=False

time: 57.2 us -> 55 us (0.962)
  Pallas kernels: 53.1 us -> 50.8 us
    pallas_call x1, Pallas kernels: 53.1 us -> 50.8 us  [local_fused(): pl.pallas_call(functools.partial(fused_kernel, tiers, groups), out_shape=...]
where the time goes in v2:
time: 55 us; the launch traced here: 54.8 us
  Pallas kernels  50.8 us (92%)
  local copies, waits for them, and re-layouts  3.34 us (6%)
  between operations  0.64 us (1%)
    pallas_call x1, Pallas kernels, local_fused(): pl.pallas_call(functools.partial(fused_kernel, tiers, groups), out_shape=...  50.8 us
    unnamed x2, local copies, waits for them, and re-layouts  3.34 us

profile of v2, /device:TPU:0, one launch (start us, length us, event | category | flops | bytes accessed | tf_op | source)
XLA Modules:
  0.0 54.8 jit_solution(10754274092387034196)
XLA Ops:
  0.6 50.8 %shard_map.59 = (bf16[128,1024]{1,0:T(8,128)(2,1)}, bf16[128,1024]{1,0:T(8,128)(2,1)}) custom-call(bf16[128,1664]{1,0:T(8,128)(2,1)} %bitcast.7, bf16[3,1664,1024]{2,1,0:T(8,128)(2,1)} %bitcast.6, s32[1,512]{1,0:T(1,128)} %seg_ref.1, s32[1,4]{1,0:T(1,128)} %flag_ref.1), custom_call_target="tpu_custom_call" | custom-call | tf_op jit(solution)/shard_map/pallas_call | solution.py:293
  51.5 1.7 %copy.8 = bf16[1,128,1024]{2,1,0:T(8,128)(2,1)} copy(bf16[1,128,1024]{2,1,0:T(8,128)(2,1)} %bitcast.9) | data formatting | bytes 524288
  53.1 1.7 %copy.9 = bf16[1,128,1024]{2,1,0:T(8,128)(2,1)} copy(bf16[1,128,1024]{2,1,0:T(8,128)(2,1)} %bitcast.8) | data formatting | bytes 524288

commit v3 on v1

--- a/solution.py
+++ b/solution.py
@@ -66,7 +66,7 @@
     pl.semaphore_wait(barrier, groups + jnp.minimum(z, 1) + jnp.minimum(tiers - 1 - z, 1))
 
     def part(c):
-        return pl.ds(c * piece, piece)
+        return pl.ds(pl.multiple_of(c * piece, piece), piece)
 
     def upward(src, t, c):
         return remote(
@@ -88,28 +88,26 @@
         def _():
             downward(x_ref.at[part(c)], z, c).start()
 
-    def relay(d):
-        for c in range(CHUNKS):
-
-            @pl.when(z - d >= 0)
-            def _():
-                t = z - d
-                src = hid.at[t, part(c)]
-                upward(src, t, c).wait_recv()
-
-                @pl.when(z < tiers - 1)
-                def _():
-                    upward(src, t, c).start()
-
-            @pl.when(z + d < tiers)
-            def _():
-                t = z + d
-                src = hid.at[t, part(c)]
-                downward(src, t, c).wait_recv()
-
-                @pl.when(z > 0)
-                def _():
-                    downward(src, t, c).start()
+    def relay(d, c):
+        @pl.when(z - d >= 0)
+        def _():
+            t = z - d
+            src = hid.at[t, part(c)]
+            upward(src, t, c).wait_recv()
+
+            @pl.when(z < tiers - 1)
+            def _():
+                upward(src, t, c).start()
+
+        @pl.when(z + d < tiers)
+        def _():
+            t = z + d
+            src = hid.at[t, part(c)]
+            downward(src, t, c).wait_recv()
+
+            @pl.when(z > 0)
+            def _():
+                downward(src, t, c).start()
 
     near = jnp.minimum(z, tiers - 1 - z)
 
@@ -120,58 +118,64 @@
         single = jnp.where(z <= tiers - 1 - z, z + far, z - far)
         return jnp.where(s <= 2 * near, paired, single)
 
-    def scatter(j, t):
-        return remote(
-            sendb.at[j - 1, t], recvb.at[j - 1, t], rs_send.at[j - 1, t], rs_recv.at[j - 1, t],
+    def scatter(j, t, c):
+        return remote(
+            sendb.at[j - 1, t, part(c)], recvb.at[j - 1, t, part(c)],
+            rs_send.at[j - 1, t, c], rs_recv.at[j - 1, t, c],
             {"mp": (m + j) % groups},
         )
 
-    def multiply(s, t):
+    def multiply(n, t, c):
         @pl.loop(1, groups)
         def _(j):
-            @pl.when(s == 0)
+            @pl.when(n == 0)
             def _():
                 weights(j).wait()
 
-            for c in range(3):
-                got = jnp.dot(hid[t], wbuf[j, c], preferred_element_type=jnp.float32)
-                sendb[j - 1, t, :, c * cols : (c + 1) * cols] = got.astype(jnp.bfloat16)
-            scatter(j, t).start()
-
-        @pl.when(s == 0)
+            for k in range(3):
+                got = jnp.dot(
+                    hid[t, part(c), :], wbuf[j, k], preferred_element_type=jnp.float32
+                )
+                sendb[j - 1, t, part(c), k * cols : (k + 1) * cols] = got.astype(jnp.bfloat16)
+            scatter(j, t, c).start()
+
+        @pl.when(n == 0)
         def _():
             weights(0).wait()
 
-        for c in range(3):
-            acc[t, :, c * cols : (c + 1) * cols] = jnp.dot(
-                hid[t], wbuf[0, c], preferred_element_type=jnp.float32
+        for k in range(3):
+            acc[t, part(c), k * cols : (k + 1) * cols] = jnp.dot(
+                hid[t, part(c), :], wbuf[0, k], preferred_element_type=jnp.float32
             )
 
-    def finish(t):
+    def finish(t, c):
         for j in range(1, groups):
-            scatter(j, t).wait_recv()
-        for c in range(3):
-            span = slice(c * cols, (c + 1) * cols)
-            value = acc[t, :, span]
+            scatter(j, t, c).wait_recv()
+        for k in range(3):
+            span = slice(k * cols, (k + 1) * cols)
+            value = acc[t, part(c), span]
             for j in range(1, groups):
-                value = value + recvb[j - 1, t, :, span].astype(jnp.float32)
-            qkv[c, pl.ds(pl.multiple_of(t * rows, rows), rows), :] = value.astype(jnp.bfloat16)
+                value = value + recvb[j - 1, t, part(c), span].astype(jnp.float32)
+            first = pl.multiple_of(t * rows + c * piece, piece)
+            qkv[k, pl.ds(first, piece), :] = value.astype(jnp.bfloat16)
 
     own.wait()
 
-    @pl.loop(0, tiers)
-    def _(s):
+    @pl.loop(0, tiers * CHUNKS)
+    def _(n):
+        s, c = n // CHUNKS, n % CHUNKS
+
         @pl.when(s > 0)
         def _():
-            relay(s)
-
-        multiply(s, shard_at(s))
-
-        @pl.when(s > 0)
-        def _():
-            finish(shard_at(s - 1))
-
-    finish(shard_at(tiers - 1))
+            relay(s, c)
+
+        multiply(n, shard_at(s), c)
+
+        @pl.when(n > 0)
+        def _():
+            finish(shard_at((n - 1) // CHUNKS), (n - 1) % CHUNKS)
+
+    finish(shard_at(tiers - 1), CHUNKS - 1)
 
     def exchange(j):
         return remote(
@@ -242,7 +246,8 @@
 
     for j in range(1, groups):
         for t in range(tiers):
-            scatter(j, t).wait_send()
+            for c in range(CHUNKS):
+                scatter(j, t, c).wait_send()
         exchange(j).wait_send()
     for j in range(1, groups + 1):
         hand(j, m, outb.at[groups - 1]).wait()
@@ -283,15 +288,15 @@
             dma((tiers, CHUNKS)),
             dma((tiers, CHUNKS)),
             dma((tiers, CHUNKS)),
-            dma((groups - 1, tiers)),
-            dma((groups - 1, tiers)),
+            dma((groups - 1, tiers, CHUNKS)),
+            dma((groups - 1, tiers, CHUNKS)),
             dma((groups - 1,)),
             dma((groups - 1,)),
             dma((groups,)),
             dma((groups,)),
         ],
         compiler_params=pltpu.CompilerParams(
-            collective_id=0, has_side_effects=True, vmem_limit_bytes=60 * 1024 * 1024
+            collective_id=0, has_side_effects=True, vmem_limit_bytes=51 * 1024 * 1024
         ),
     )(rows, weights, segment_ids, exit_flags)
     return (attended[None], handed[None])

time: 57.2 us -> 54 us (0.944)
  Pallas kernels: 53.1 us -> 49.4 us
    pallas_call x1, Pallas kernels: 53.1 us -> 49.4 us  [local_fused(): pl.pallas_call(functools.partial(fused_kernel, tiers, groups), out_shape=...]
    unnamed x2 -> x8, local copies, waits for them, and re-layouts: 3.34 us -> 3.74 us
where the time goes in v3:
time: 54 us; the launch traced here: 53.8 us
  Pallas kernels  49.4 us (91%)
  local copies, waits for them, and re-layouts  3.74 us (7%)
  between operations  0.65 us (1%)
    pallas_call x1, Pallas kernels, local_fused(): pl.pallas_call(functools.partial(fused_kernel, tiers, groups), out_shape=...  49.4 us
    unnamed x8, local copies, waits for them, and re-layouts  3.74 us

profile of v3, /device:TPU:0, one launch (start us, length us, event | category | flops | bytes accessed | tf_op | source)
XLA Modules:
  0.0 53.8 jit_solution(9332413841467300948)
XLA Ops:
  0.6 0.0 copy-start
  0.6 1.0 %copy-done = bf16[1,128,1664]{2,1,0:T(8,128)(2,1)S(1)} copy-done((bf16[1,128,1664]{2,1,0:T(8,128)(2,1)S(1)}, bf16[1,128,1664]{2,1,0:T(8,128)(2,1)}, u32[]{:S(2)}) %copy-start) | copy-done | bytes 426008
  1.6 0.0 copy-start.1
  1.6 0.7 %copy-done.1 = s32[1,512]{1,0:T(1,128)S(1)} copy-done((s32[1,512]{1,0:T(1,128)S(1)}, s32[1,512]{1,0:T(1,128)}, u32[]{:S(2)}) %copy-start.1) | copy-done | bytes 2072
  2.3 0.0 copy-start.2
  2.3 0.7 %copy-done.2 = s32[1,4]{1,0:T(1,128)S(1)} copy-done((s32[1,4]{1,0:T(1,128)S(1)}, s32[1,4]{1,0:T(1,128)}, u32[]{:S(2)}) %copy-start.2) | copy-done | bytes 40
  3.0 49.4 %shard_map.59 = (bf16[128,1024]{1,0:T(8,128)(2,1)S(1)}, bf16[128,1024]{1,0:T(8,128)(2,1)S(1)}) custom-call(bf16[128,1664]{1,0:T(8,128)(2,1)S(1)} %bitcast.6, bf16[3,1664,1024]{2,1,0:T(8,128)(2,1)} %bitcast.9, s32[1,512]{1,0:T(1,128)S(1)} %copy-done.1, s32[1,4]{1,0:T(1,128)S(1)} %copy-done.2), custom_call_target="tpu_custom_call" | custom-call | tf_op jit(solution)/shard_map/pallas_call | solution.py:268
  52.4 0.7 %copy.8 = bf16[1,128,1024]{2,1,0:T(8,128)(2,1)} copy(bf16[1,128,1024]{2,1,0:T(8,128)(2,1)S(1)} %bitcast.8) | data formatting | bytes 524288
  53.1 0.7 %copy.9 = bf16[1,128,1024]{2,1,0:T(8,128)(2,1)} copy(bf16[1,128,1024]{2,1,0:T(8,128)(2,1)S(1)} %bitcast.7) | data formatting | bytes 524288
Async XLA Ops:
  0.6 1.0 %copy-start = (bf16[1,128,1664]{2,1,0:T(8,128)(2,1)S(1)}, bf16[1,128,1664]{2,1,0:T(8,128)(2,1)}, u32[]{:S(2)}) copy-start(bf16[1,128,1664]{2,1,0:T(8,128)(2,1)} %param.4) | copy-start | bytes 1277956
  1.6 0.7 %copy-start.1 = (s32[1,512]{1,0:T(1,128)S(1)}, s32[1,512]{1,0:T(1,128)}, u32[]{:S(2)}) copy-start(s32[1,512]{1,0:T(1,128)} %seg_ref.1) | copy-start | bytes 6148
  2.3 0.7 %copy-start.2 = (s32[1,4]{1,0:T(1,128)S(1)}, s32[1,4]{1,0:T(1,128)}, u32[]{:S(2)}) copy-start(s32[1,4]{1,0:T(1,128)} %flag_ref.1) | copy-start | bytes 52
